TPU v7x, 512 devices: a whole 4x8x8 slice. The times are simulated.
512 devices in a mesh: chan: 8 (over z), space: 64 (over y, x, core).
Axes of the slice: x: 4, y: 8, z: 8, core: 2. Of those that a mesh axis runs over, the one named last changes fastest.
Arguments:
- cotangent: bfloat16 [80, 131072], P(None, 'space'), may hold values from -6 to 6
- pair_band: int32 [8192], P('space'), may hold values from 0 to 15
- pair_target: int32 [8192], P('space'), may hold values from 0 to 1023, as said below
- pair_count: int32 [64], P('space'), may hold values from 1 to 128, as said below
- pair_weight: bfloat16 [8192, 128, 128], P('space'), may hold values from -0.5 to 0.5
- head_weight: bfloat16 [512, 80], P('chan'), may hold values from -0.25 to 0.25
- features: bfloat16 [512, 131072], P('chan', 'space'), may hold values from -6 to 6
Outputs:
- feature_grad: bfloat16 [512, 131072], P('chan', 'space')
- weight_grad: float32 [512, 80], P('chan')
Inputs may be any that keep to these rules, and one draw needn't show every extreme that they name: `pair_target`: targets of the slots of one device fall on each device's blocks (device index = target // 16) exactly 2 times, so at most 2 live pairs go from one device to one device; the first and last device of space have all slots live. `pair_count`: devices near both ends of space carry more live pairs than those in the middle.
All inputs are finite; a program needn't handle non-finite values.
Results may differ from a plain program's by a relative error of at most 0.0058.
Values may be sent and summed in bfloat16 or wider, within the bound.
No kernel may reach another device: no remote copies, remote signals or barrier semaphores. Data moves between devices by JAX's collectives and lax.ppermute only.
A program may use at most 64 MiB of HBM per device.

v0:
```python
import jax
import jax.numpy as jnp
from jax import lax
from jax.sharding import PartitionSpec as P


def on_device(cotangent, pair_band, pair_target, pair_count, pair_weight, head_weight, features):
    nspace = lax.axis_size("space")
    vars_all = cotangent.shape[0]
    ll_local = cotangent.shape[1]
    block_size = pair_weight.shape[1]
    pair_slots = pair_band.shape[0]
    hp_local = features.shape[1]
    hp_blocks = hp_local // block_size
    per_peer = pair_slots // nspace
    band_blocks = cotangent.reshape(vars_all, ll_local // block_size, block_size).transpose(1, 0, 2)
    picked = band_blocks[pair_band]
    contrib = jnp.einsum(
        "pvr,prq->pvq", picked, pair_weight, preferred_element_type=jnp.float32
    ).astype(jnp.bfloat16)
    pair_index = jnp.arange(pair_slots)
    live_pair = pair_index < pair_count[0]
    dest_device = pair_target // hp_blocks
    local_block = pair_target % hp_blocks
    earlier = (
        (dest_device[:, None] == dest_device[None, :])
        & live_pair[None, :]
        & (pair_index[None, :] < pair_index[:, None])
    )
    slot_rank = jnp.sum(earlier.astype(jnp.int32), axis=1)
    slot_index = jnp.where(live_pair, dest_device * per_peer + slot_rank, pair_slots)
    sendbuf = (
        jnp.zeros((pair_slots, vars_all, block_size), jnp.bfloat16)
        .at[slot_index]
        .set(contrib, mode="drop")
    )
    labels = (
        jnp.full((pair_slots,), -1.0, jnp.bfloat16)
        .at[slot_index]
        .set(local_block.astype(jnp.bfloat16), mode="drop")
    )
    sendbuf = sendbuf.reshape(nspace, per_peer, vars_all, block_size)
    labels = labels.reshape(nspace, per_peer)
    received, received_tags = (
        lax.all_to_all(sendbuf, "space", split_axis=0, concat_axis=0, tiled=True),
        lax.all_to_all(labels, "space", split_axis=0, concat_axis=0, tiled=True),
    )
    block_ids = jnp.arange(hp_blocks).astype(jnp.bfloat16)
    onehot = (received_tags.reshape(pair_slots)[:, None] == block_ids[None, :]).astype(jnp.bfloat16)
    summed = jnp.einsum(
        "sh,svq->vhq",
        onehot,
        received.reshape(pair_slots, vars_all, block_size),
        preferred_element_type=jnp.float32,
    )
    pixel_part = summed.astype(jnp.bfloat16).reshape(vars_all, hp_local)
    feature_grad = jnp.dot(head_weight, pixel_part, preferred_element_type=jnp.float32).astype(
        jnp.bfloat16
    )
    partial_value = lax.dot_general(
        features, pixel_part, (((1,), (1,)), ((), ())), preferred_element_type=jnp.float32
    )
    grad_scale = float(hp_local * nspace) ** (-0.5)
    weight_grad = lax.psum(partial_value, "space") * grad_scale
    return (feature_grad, weight_grad)


def solution(mesh):
    placed = (
        P(None, "space"),
        P("space"),
        P("space"),
        P("space"),
        P("space", None, None),
        P("chan", None),
        P("chan", "space"),
    )
    return jax.shard_map(
        on_device,
        mesh=mesh,
        in_specs=placed,
        out_specs=(P("chan", "space"), P("chan", None)),
        check_vma=False,
    )
```

profile of v0, /device:TPU:256, one launch (start us, length us, event | category | flops | bytes accessed | tf_op | source)
XLA Modules:
  0.0 362.7 jit_solution(4748789527923973483)
XLA Ops:
  0.6 0.0 copy-start
  0.6 0.7 fusion.10
  2.0 0.2 convert_reduce_fusion
  2.2 1.3 scatter_custom_fusion.1
  3.6 0.8 all_to_all.12
  4.4 10.6 %all-to-all-start.1 = ((bf16[64,1,2]{2,1,0:T(2,128)(2,1)}), bf16[64,1,2]{2,1,0:T(2,128)(2,1)S(1)}, u32[]{:S(2)}, u32[]{:S(2)}) async-start(bf16[64,1,2]{2,1,0:T(2,128)(2,1)} %all_to_all.12), calls=%async_computation.1 | async-start | bytes 65536 | tf_op jit(solution)/shard_map/all_to_all | solution.py:46
  14.9 0.0 copy-done
  14.9 0.1 bitcast_bitcast_fusion
  15.0 0.7 compare_select_fusion
  15.7 1.1 gather_fusion
  16.7 5.2 %convolution_convert_fusion.1 = bf16[128,80,128]{2,1,0:T(8,128)(2,1)} fusion(bf16[128,80,128]{2,1,0:T(8,128)(2,1)S(1)} %gather_fusion, bf16[128,128,128]{2,1,0:T(8,128)(2,1)} %param.11), kind=kOutput, calls=%fused_computation.5 | convolution fusion | flops 336855040 | bytes 9437184 | tf_op jit(solution)/shard_map/pvr,prq->pvq/dot_general | solution.py:18
  22.0 0.3 broadcast_in_dim.12
  22.3 12.1 %scatter_fusion = bf16[128,80,128]{2,1,0:T(8,128)(2,1)S(1)} fusion(bf16[128,80,128]{2,1,0:T(8,128)(2,1)S(1)} %broadcast_in_dim.12, s32[128]{0:T(128)S(1)} %compare_select_fusion.1, bf16[128,80,128]{2,1,0:T(8,128)(2,1)} %convolution_convert_fusion.1), kind=kCustom, calls=%fused_computation.1 | custom fusion | bytes 7864832 | tf_op jit(solution)/shard_map/scatter | solution.py:35
  34.5 3.6 copy.17
  38.0 0.0 all-to-all-done.1
  38.0 10.5 %all-to-all-start = ((bf16[64,2,80,128]{3,1,2,0:T(2,128)(2,1)}), bf16[64,2,80,128]{3,1,2,0:T(2,128)(2,1)S(1)}, u32[]{:S(2)}, u32[]{:S(2)}) async-start(bf16[64,2,80,128]{3,1,2,0:T(2,128)(2,1)} %copy.17), calls=%async_computation | async-start | bytes 5242880 | tf_op jit(solution)/shard_map/all_to_all | solution.py:45
  48.5 0.1 reduce
  48.6 0.1 eq.33
  48.8 62.3 %all-to-all-done = bf16[64,2,80,128]{3,1,2,0:T(2,128)(2,1)S(1)} async-done(((bf16[64,2,80,128]{3,1,2,0:T(2,128)(2,1)}), bf16[64,2,80,128]{3,1,2,0:T(2,128)(2,1)S(1)}, u32[]{:S(2)}, u32[]{:S(2)}) %all-to-all-start) | async-done | bytes 2621472 | tf_op jit(solution)/shard_map/all_to_all | solution.py:45
  111.1 2.9 copy.18
  114.0 0.0 copy-start.1
  114.0 0.0 copy-start.2
  114.0 0.5 convolution_convert_fusion.2
  114.6 0.2 copy-done.1
  114.7 0.9 fusion
  115.7 0.0 copy-done.2
  115.7 0.2 convolution_bitcast_fusion
  115.9 246.1 %psum.7 = f32[64,80]{1,0:T(8,128)S(1)} all-reduce(f32[64,80]{1,0:T(8,128)S(1)} %convolution_bitcast_fusion), channel_id=1, replica_groups=mesh['chan'=8,'space'=64] {'space'}, use_global_device_ids=true, to_apply=%region_3.4 | all-reduce | flops 5120 | bytes 40960 | tf_op jit(solution)/shard_map/psum | solution.py:64
  362.1 0.6 broadcast_multiply_fusion
  (4 shorter events, 0.0 us)
Async XLA Ops:
  0.6 14.3 %copy-start = (bf16[80,2048]{1,0:T(8,128)(2,1)S(1)}, bf16[80,2048]{1,0:T(8,128)(2,1)}, u32[]{:S(2)}) copy-start(bf16[80,2048]{1,0:T(8,128)(2,1)} %param.7) | copy-start | bytes 983044
  4.4 33.7 %all-to-all-start.1 = ((bf16[64,1,2]{2,1,0:T(2,128)(2,1)}), bf16[64,1,2]{2,1,0:T(2,128)(2,1)S(1)}, u32[]{:S(2)}, u32[]{:S(2)}) async-start(bf16[64,1,2]{2,1,0:T(2,128)(2,1)} %all_to_all.12), calls=%async_computation.1 | async-start | bytes 65536 | tf_op jit(solution)/shard_map/all_to_all | solution.py:46
  38.0 73.1 %all-to-all-start = ((bf16[64,2,80,128]{3,1,2,0:T(2,128)(2,1)}), bf16[64,2,80,128]{3,1,2,0:T(2,128)(2,1)S(1)}, u32[]{:S(2)}, u32[]{:S(2)}) async-start(bf16[64,2,80,128]{3,1,2,0:T(2,128)(2,1)} %copy.17), calls=%async_computation | async-start | bytes 5242880 | tf_op jit(solution)/shard_map/all_to_all | solution.py:45
  114.0 0.7 copy-start.1
  114.0 1.6 copy-start.2
where the time goes:
time: 363 us
  blocking collectives  246 us (68%)
  waiting for transfers between devices  62.4 us (17%)
  local copies, waits for them, and re-layouts  22.6 us (6%)
  starting transfers between devices  21 us (6%)
  matrix products  6.89 us (2%)
    psum x1, blocking collectives, on_device(): weight_grad = lax.psum(partial_value, 'space') * grad_scale  246 us
    all_to_all x1, waiting for transfers between devices, on_device(): lax.all_to_all(sendbuf, 'space', split_axis=0, concat_axis=0, tiled=True)  62.3 us
    scatter x1, local copies, waits for them, and re-layouts, on_device(): sendbuf = jnp.zeros((pair_slots, vars_all, block_size), jnp.bfloat16).at[...  12.1 us
    all_to_all x1, starting transfers between devices, on_device(): lax.all_to_all(labels, 'space', split_axis=0, concat_axis=0, tiled=True)  10.6 us
    all_to_all x1, starting transfers between devices, on_device(): lax.all_to_all(sendbuf, 'space', split_axis=0, concat_axis=0, tiled=True)  10.5 us
  transfers between devices with their start and end apart: 2, of which 1 were waited for; matrix products, arithmetic and copies ran while one was open for 6% of the time, Pallas kernels for 0%

commit v1 on v0

--- a/solution.py
+++ b/solution.py
@@ -2,6 +2,11 @@
 import jax.numpy as jnp
 from jax import lax
 from jax.sharding import PartitionSpec as P
+
+
+def gather_and_add(shard, axis):
+    parts = lax.all_gather(shard, axis)
+    return jnp.sum(parts, axis=0)
 
 
 def on_device(cotangent, pair_band, pair_target, pair_count, pair_weight, head_weight, features):
@@ -61,7 +66,7 @@
         features, pixel_part, (((1,), (1,)), ((), ())), preferred_element_type=jnp.float32
     )
     grad_scale = float(hp_local * nspace) ** (-0.5)
-    weight_grad = lax.psum(partial_value, "space") * grad_scale
+    weight_grad = gather_and_add(partial_value, "space") * grad_scale
     return (feature_grad, weight_grad)
 
 

time: 363 us -> 216 us (0.60)
  the two profiles are of different devices: /device:TPU:256 before, /device:TPU:1 now
where the time goes in v1:
time: 216 us; the launch traced here: 215 us
  waiting for transfers between devices  144 us (67%)
  local copies, waits for them, and re-layouts  22.8 us (11%)
  starting transfers between devices  22.1 us (10%)
  between operations  14.8 us (7%)
  matrix products  7.5 us (3%)
  other arithmetic  4.06 us (2%)
    all_gather x1, waiting for transfers between devices, gather_and_add(): parts = lax.all_gather(shard, axis)  83.2 us
    all_to_all x1, waiting for transfers between devices, on_device(): lax.all_to_all(sendbuf, 'space', split_axis=0, concat_axis=0, tiled=True)  60.6 us
    scatter x1, local copies, waits for them, and re-layouts, on_device(): sendbuf = jnp.zeros((pair_slots, vars_all, block_size), jnp.bfloat16).at[...  12.2 us
    all_to_all x1, starting transfers between devices, on_device(): lax.all_to_all(labels, 'space', split_axis=0, concat_axis=0, tiled=True)  11.6 us
    all_to_all x1, starting transfers between devices, on_device(): lax.all_to_all(sendbuf, 'space', split_axis=0, concat_axis=0, tiled=True)  10.4 us
    dot_general x1, matrix products, on_device(): jnp.einsum('pvr,prq->pvq', picked, pair_weight, preferred_element_type=jn...  5.22 us
  transfers between devices with their start and end apart: 3, of which 2 were waited for; matrix products, arithmetic and copies ran while one was open for 11% of the time, Pallas kernels for 0%

profile of v1, /device:TPU:1, one launch (start us, length us, event | category | flops | bytes accessed | tf_op | source)
XLA Modules:
  0.0 215.0 jit_solution(2081098586910395095)
XLA Ops:
  7.2 0.0 copy-start
  7.2 0.7 fusion.10
  8.6 0.2 convert_reduce_fusion
  8.7 1.3 scatter_custom_fusion.1
  10.1 0.8 all_to_all.12
  10.9 11.6 %all-to-all-start.1 = ((bf16[64,1,2]{2,1,0:T(2,128)(2,1)}), bf16[64,1,2]{2,1,0:T(2,128)(2,1)S(1)}, u32[]{:S(2)}, u32[]{:S(2)}) async-start(bf16[64,1,2]{2,1,0:T(2,128)(2,1)} %all_to_all.12), calls=%async_computation.1 | async-start | bytes 65536 | tf_op jit(solution)/shard_map/all_to_all | solution.py:51
  22.5 0.0 copy-done
  22.5 0.1 bitcast_bitcast_fusion
  22.6 0.7 compare_select_fusion
  23.2 1.1 gather_fusion
  24.3 5.2 %convolution_convert_fusion.1 = bf16[128,80,128]{2,1,0:T(8,128)(2,1)} fusion(bf16[128,80,128]{2,1,0:T(8,128)(2,1)S(1)} %gather_fusion, bf16[128,128,128]{2,1,0:T(8,128)(2,1)} %param.11), kind=kOutput, calls=%fused_computation.5 | convolution fusion | flops 336855040 | bytes 9437184 | tf_op jit(solution)/shard_map/pvr,prq->pvq/dot_general | solution.py:23
  29.5 0.3 broadcast_in_dim.12
  29.9 12.2 %scatter_fusion = bf16[128,80,128]{2,1,0:T(8,128)(2,1)S(1)} fusion(bf16[128,80,128]{2,1,0:T(8,128)(2,1)S(1)} %broadcast_in_dim.12, s32[128]{0:T(128)S(1)} %compare_select_fusion.1, bf16[128,80,128]{2,1,0:T(8,128)(2,1)} %convolution_convert_fusion.1), kind=kCustom, calls=%fused_computation.1 | custom fusion | bytes 7864832 | tf_op jit(solution)/shard_map/scatter | solution.py:40
  42.0 3.6 %copy.17 = bf16[64,2,80,128]{3,1,2,0:T(2,128)(2,1)} copy(bf16[64,2,80,128]{3,2,1,0:T(8,128)(2,1)S(1)} %bitcast.32) | data formatting | bytes 5242880 | tf_op jit(solution)/shard_map/reshape | solution.py:47
  45.6 0.0 all-to-all-done.1
  45.6 10.4 %all-to-all-start = ((bf16[64,2,80,128]{3,1,2,0:T(2,128)(2,1)}), bf16[64,2,80,128]{3,1,2,0:T(2,128)(2,1)S(1)}, u32[]{:S(2)}, u32[]{:S(2)}) async-start(bf16[64,2,80,128]{3,1,2,0:T(2,128)(2,1)} %copy.17), calls=%async_computation | async-start | bytes 5242880 | tf_op jit(solution)/shard_map/all_to_all | solution.py:50
  56.1 0.0 all-gather.3.cloned.1.call-start
  56.1 0.1 reduce
  56.2 0.1 eq.33
  56.4 60.6 %all-to-all-done = bf16[64,2,80,128]{3,1,2,0:T(2,128)(2,1)S(1)} async-done(((bf16[64,2,80,128]{3,1,2,0:T(2,128)(2,1)}), bf16[64,2,80,128]{3,1,2,0:T(2,128)(2,1)S(1)}, u32[]{:S(2)}, u32[]{:S(2)}) %all-to-all-start) | async-done | bytes 2621472 | tf_op jit(solution)/shard_map/all_to_all | solution.py:50
  117.0 2.9 %copy.18 = bf16[64,2,80,128]{3,1,0,2:T(2,128)(2,1)S(1)} copy(bf16[64,2,80,128]{3,1,2,0:T(2,128)(2,1)S(1)} %all-to-all-done) | data formatting | bytes 5242880 | tf_op jit(solution)/shard_map/all_to_all | solution.py:50
  119.9 0.0 copy-start.2
  119.9 0.0 copy-start.1
  119.9 0.5 convolution_convert_fusion.2
  120.4 0.4 copy-done.2
  120.8 0.9 convolution_bitcast_fusion
  121.7 0.0 all-gather.3.cloned.1.call-update
  121.7 0.0 copy-done.1
  121.7 0.9 fusion
  122.6 83.2 %all-gather.3.cloned.1.call-done = f32[4096,80]{1,0:T(8,128)} async-done(((f32[64,80]{1,0:T(8,128)}), f32[4096,80]{1,0:T(8,128)}) %all-gather.3.cloned.1.call-update) | async-done | bytes 1310736 | tf_op jit(solution)/shard_map/all_gather | solution.py:8
  205.8 1.8 reduce_sum.19
  207.6 0.6 broadcast_multiply_fusion
  (4 shorter events, 0.0 us)
Async XLA Ops:
  7.2 15.3 %copy-start = (bf16[80,2048]{1,0:T(8,128)(2,1)S(1)}, bf16[80,2048]{1,0:T(8,128)(2,1)}, u32[]{:S(2)}) copy-start(bf16[80,2048]{1,0:T(8,128)(2,1)} %param.7) | copy-start | bytes 983044
  10.9 34.7 %all-to-all-start.1 = ((bf16[64,1,2]{2,1,0:T(2,128)(2,1)}), bf16[64,1,2]{2,1,0:T(2,128)(2,1)S(1)}, u32[]{:S(2)}, u32[]{:S(2)}) async-start(bf16[64,1,2]{2,1,0:T(2,128)(2,1)} %all_to_all.12), calls=%async_computation.1 | async-start | bytes 65536 | tf_op jit(solution)/shard_map/all_to_all | solution.py:51
  45.6 71.3 %all-to-all-start = ((bf16[64,2,80,128]{3,1,2,0:T(2,128)(2,1)}), bf16[64,2,80,128]{3,1,2,0:T(2,128)(2,1)S(1)}, u32[]{:S(2)}, u32[]{:S(2)}) async-start(bf16[64,2,80,128]{3,1,2,0:T(2,128)(2,1)} %copy.17), calls=%async_computation | async-start | bytes 5242880 | tf_op jit(solution)/shard_map/all_to_all | solution.py:50
  56.1 149.7 %all-gather.3.cloned.1.call-start = ((), (), s32[]{:S(2)}) async-start(), calls=%async_computation.2 | async-start | bytes 2129920 | tf_op jit(solution)/shard_map/all_gather | solution.py:8
  119.9 1.0 copy-start.2
  119.9 1.8 copy-start.1
Sparse Core Ops, SparseCore 0:
  121.8 83.9 all-gather.2
